TPU v7x, 256 devices: a whole 4x4x8 slice. The times are simulated.
256 devices in a mesh: tm: 8 (over x_hi, y), azim: 32 (over z, x_lo, core).
Axes of the slice: x: 4 (x_hi: 2, x_lo: 2; x = x_hi * 2 + x_lo), y: 4, z: 8, core: 2. Of those that a mesh axis runs over, the one named last changes fastest.
Arguments:
- rotor_coeffs: float32 [64, 2, 32, 16384], P('tm', None, 'azim'), may hold values from -1.5 to 1.5
- mortar_weights: float32 [64, 2, 32, 16384], P('tm', None, 'azim'), may hold values from 0.2 to 1
- block_shifts: int32 [64], P('tm'), may hold values from 0 to 31
- stencil_offsets: int32 [64, 2], P('tm'), may hold values from -1 to 1
- reluctivity: float32 [32, 16384], P('azim'), may hold values from 0.5 to 2
- source: float32 [64, 2, 32, 16384], P('tm', None, 'azim'), may hold values from -3 to 3
Outputs:
- residual: float32 [64, 2, 32, 16384], P('tm', None, 'azim')
All inputs are finite; a program needn't handle non-finite values.
Results may differ from a plain program's by a relative error of at most 0.0001.
Values sent between devices are 32-bit elements; how exact they have to be, the bound alone decides.
A program may use at most 128 MiB of HBM per device.

v0:
```python
import itertools
import jax
import jax.numpy as jnp
import numpy as np
from jax import lax
from jax.sharding import PartitionSpec as P

KC = 64
NT = 64
LANES = 128


def shifted(value, axis, steps):
    count = lax.axis_size(axis)
    pairs = [(source, (source + steps) % count) for source in range(count)]
    return lax.ppermute(value, axis, pairs)


def harmonic_basis(sample_rows, coefficient_count):
    column = jnp.arange(coefficient_count, dtype=jnp.int32)
    harmonic_order = 2 * (column // 2) + 1
    phase_index = harmonic_order[None, :] * (2 * sample_rows[:, None] + 1) % (4 * NT)
    phase_angle = phase_index.astype(jnp.float32) * (jnp.pi / (2 * NT))
    return jnp.where(column[None, :] % 2 == 0, jnp.cos(phase_angle), jnp.sin(phase_angle))


def per_sample(flags, value):
    return flags.reshape((-1,) + (1,) * (value.ndim - 1))


def digit_table(stages, count):
    found = {}
    for bits in itertools.product((0, 1), repeat=len(stages)):
        found.setdefault(sum((b * s for b, s in zip(bits, stages))) % count, bits)
    return np.array([found[d] for d in range(count)], np.int32)


def barrel(value, amounts, stages, axis):
    count = lax.axis_size(axis)
    picks = jnp.take(jnp.asarray(digit_table(stages, count)), amounts % count, axis=0)
    for level, steps in enumerate(stages):
        moved = shifted(value, axis, steps)
        value = jnp.where(per_sample(picks[:, level] == 1, value), moved, value)
    return value


def body(rotor_coeffs, mortar_weights, block_shifts, stencil_offsets, reluctivity, source):
    local_c, comp, _, nodes = rotor_coeffs.shape
    local_j, sten = mortar_weights.shape[:2]
    rows = nodes // LANES
    parts = lax.axis_size("tm")
    chunk = rows // parts
    coeffs = lax.all_to_all(
        rotor_coeffs.reshape(local_c, comp, rows, LANES),
        "tm",
        split_axis=2,
        concat_axis=0,
        tiled=True,
    )
    weights = lax.all_to_all(
        mortar_weights.reshape(local_j, sten, rows, LANES),
        "tm",
        split_axis=2,
        concat_axis=0,
        tiled=True,
    )
    small = jnp.concatenate([block_shifts[:, None], stencil_offsets], axis=1).astype(jnp.float32)
    small = lax.all_gather(small, "tm", tiled=True).astype(jnp.int32)
    shifts, offsets = (small[:, 0], small[:, 1:])
    gain = lax.dynamic_slice_in_dim(
        reluctivity.reshape(rows, LANES), lax.axis_index("tm") * chunk, chunk, axis=0
    )
    table = harmonic_basis(jnp.arange(NT, dtype=jnp.int32), KC)
    samples = jnp.einsum("jc,capk->japk", table, coeffs, precision=lax.Precision.HIGHEST)
    orders = ((1, 2, 4, -8, 16), (16, 8, -4, 2, 1))
    fields = []
    for component in range(comp):
        turned = barrel(samples[:, component], shifts, orders[component % 2], "azim")
        from_left = shifted(turned, "azim", 1)
        from_right = shifted(turned, "azim", -1)
        field = jnp.zeros_like(turned)
        for stencil_entry in range(sten):
            offset = offsets[:, stencil_entry]
            neighbour = jnp.where(
                per_sample(offset == 0, turned),
                turned,
                jnp.where(per_sample(offset > 0, turned), from_right, from_left),
            )
            field = field + weights[:, stencil_entry] * neighbour
        fields.append(field)
    airgap_field = jnp.stack(fields, axis=1)
    square = jnp.sum(airgap_field * airgap_field, axis=1, keepdims=True)
    field_flux = gain[None, None] * (1.0 + square / (1.0 + square)) * airgap_field
    summed = jnp.einsum(
        "jc,japk->capk", table * (2.0 / NT), field_flux, precision=lax.Precision.HIGHEST
    )
    residual = lax.all_to_all(summed, "tm", split_axis=0, concat_axis=2, tiled=True)
    return residual.reshape(source.shape) - source


def solution(mesh):
    in_specs = (
        P("tm", None, "azim", None),
        P("tm", None, "azim", None),
        P("tm"),
        P("tm", None),
        P("azim", None),
        P("tm", None, "azim", None),
    )
    out_specs = P("tm", None, "azim", None)
    return jax.shard_map(body, mesh=mesh, in_specs=in_specs, out_specs=out_specs, check_vma=False)
```

profile of v0, /device:TPU:1, one launch (start us, length us, event | category | flops | bytes accessed | tf_op | source)
XLA Modules:
  0.0 249.5 jit_solution(8012935296902372771)
XLA Ops:
  0.0 3.0 %copy.42 = f32[8,2,128,128]{3,1,0,2:T(2,128)} copy(f32[8,2,128,128]{3,2,1,0:T(8,128)} %bitcast.73) | data formatting | bytes 2097152 | tf_op jit(solution)/shard_map/reshape | solution.py:54
  3.0 7.5 %all-to-all-start.1 = ((f32[8,2,128,128]{3,1,0,2:T(2,128)}), f32[8,2,128,128]{3,1,0,2:T(2,128)S(1)}, u32[]{:S(2)}, u32[]{:S(2)}) async-start(f32[8,2,128,128]{3,1,0,2:T(2,128)} %copy.42), calls=%async_computation.1 | async-start | bytes 2097152 | tf_op jit(solution)/shard_map/all_to_all | solution.py:53
  11.2 34.0 %all-gather = f32[8,8,3]{1,2,0:T(4,128)S(1)} all-gather(f32[1,8,3]{1,2,0:T(4,128)S(1)} %fusion.25), channel_id=1, replica_groups=mesh['tm'=8,'azim'=32] {'tm'}, dimensions={0}, use_global_device_ids=true | all-gather | bytes 864 | tf_op jit(solution)/shard_map/all_gather | solution.py:68
  45.7 1.8 fusion
  47.6 5.6 %collective-permute-start = (f32[64,16,128]{2,0,1:T(8,128)S(1)}, f32[64,16,128]{2,0,1:T(8,128)S(1)}, u32[]{:S(2)}, u32[]{:S(2)}) collective-permute-start(f32[64,16,128]{2,0,1:T(8,128)S(1)} %get-tuple-element.22), channel_id=1, source_target_pairs={{0,1},{1,2},{2,3},{3,4},{4,5},{5,6},{6,7},{7,8},{8,9},{9,10},{10,1... | collective-permute-start | bytes 1572872 | tf_op jit(solution)/shard_map/ppermute | solution.py:16
  53.2 6.9 %collective-permute-start.7 = (f32[64,16,128]{2,0,1:T(8,128)S(1)}, f32[64,16,128]{2,0,1:T(8,128)S(1)}, u32[]{:S(2)}, u32[]{:S(2)}) collective-permute-start(f32[64,16,128]{2,0,1:T(8,128)S(1)} %get-tuple-element.23), channel_id=1, source_target_pairs={{0,16},{1,17},{2,18},{3,19},{4,20},{5,21},{6,22},{7,23},{8,24},{9,... | collective-permute-start | bytes 1572872 | tf_op jit(solution)/shard_map/ppermute | solution.py:16
  62.0 12.7 %collective-permute-done.7 = f32[64,16,128]{2,0,1:T(8,128)S(1)} collective-permute-done((f32[64,16,128]{2,0,1:T(8,128)S(1)}, f32[64,16,128]{2,0,1:T(8,128)S(1)}, u32[]{:S(2)}, u32[]{:S(2)}) %collective-permute-start.7) | collective-permute-done | bytes 524320 | tf_op jit(solution)/shard_map/ppermute | solution.py:16
  74.9 7.1 %collective-permute-start.1 = (f32[64,16,128]{2,0,1:T(8,128)S(1)}, f32[64,16,128]{2,0,1:T(8,128)S(1)}, u32[]{:S(2)}, u32[]{:S(2)}) collective-permute-start(f32[64,16,128]{2,0,1:T(8,128)S(1)} %get-tuple-element.20), channel_id=1, source_target_pairs={{0,2},{1,3},{2,4},{3,5},{4,6},{5,7},{6,8},{7,9},{8,10},{9,11},{10,... | collective-permute-start | bytes 1572872 | tf_op jit(solution)/shard_map/ppermute | solution.py:16
  82.0 9.7 %collective-permute-start.8 = (f32[64,16,128]{2,0,1:T(8,128)S(1)}, f32[64,16,128]{2,0,1:T(8,128)S(1)}, u32[]{:S(2)}, u32[]{:S(2)}) collective-permute-start(f32[64,16,128]{2,0,1:T(8,128)S(1)} %get-tuple-element.21), channel_id=1, source_target_pairs={{0,8},{1,9},{2,10},{3,11},{4,12},{5,13},{6,14},{7,15},{8,16},{9,17... | collective-permute-start | bytes 1572872 | tf_op jit(solution)/shard_map/ppermute | solution.py:16
  91.7 8.9 %collective-permute-done.1 = f32[64,16,128]{2,0,1:T(8,128)S(1)} collective-permute-done((f32[64,16,128]{2,0,1:T(8,128)S(1)}, f32[64,16,128]{2,0,1:T(8,128)S(1)}, u32[]{:S(2)}, u32[]{:S(2)}) %collective-permute-start.1) | collective-permute-done | bytes 524320 | tf_op jit(solution)/shard_map/ppermute | solution.py:16
  100.7 1.0 collective-permute-start.2
  101.8 11.3 %collective-permute-done.8 = f32[64,16,128]{2,0,1:T(8,128)S(1)} collective-permute-done((f32[64,16,128]{2,0,1:T(8,128)S(1)}, f32[64,16,128]{2,0,1:T(8,128)S(1)}, u32[]{:S(2)}, u32[]{:S(2)}) %collective-permute-start.8) | collective-permute-done | bytes 524320 | tf_op jit(solution)/shard_map/ppermute | solution.py:16
  113.3 11.0 %collective-permute-done.2 = f32[64,16,128]{2,0,1:T(8,128)S(1)} collective-permute-done((f32[64,16,128]{2,0,1:T(8,128)S(1)}, f32[64,16,128]{2,0,1:T(8,128)S(1)}, u32[]{:S(2)}, u32[]{:S(2)}) %collective-permute-start.2) | collective-permute-done | bytes 524320 | tf_op jit(solution)/shard_map/ppermute | solution.py:16
  126.5 10.6 %collective-permute-start.10 = (f32[64,16,128]{2,0,1:T(8,128)S(1)}, f32[64,16,128]{2,0,1:T(8,128)S(1)}, u32[]{:S(2)}, u32[]{:S(2)}) collective-permute-start(f32[64,16,128]{2,0,1:T(8,128)S(1)} %broadcast_select_fusion.2), channel_id=1, source_target_pairs={{0,2},{1,3},{2,4},{3,5},{4,6},{5,7},{6,8},{7,9},{8,10},{9,11},{10,... | collective-permute-start | bytes 1572872 | tf_op jit(solution)/shard_map/ppermute | solution.py:16
  137.1 12.8 %collective-permute-done.3 = f32[64,16,128]{2,0,1:T(8,128)S(1)} collective-permute-done((f32[64,16,128]{2,0,1:T(8,128)S(1)}, f32[64,16,128]{2,0,1:T(8,128)S(1)}, u32[]{:S(2)}, u32[]{:S(2)}) %collective-permute-start.3) | collective-permute-done | bytes 524320 | tf_op jit(solution)/shard_map/ppermute | solution.py:16
  150.0 2.1 collective-permute-start.4
  152.3 26.2 %collective-permute-start.11 = (f32[64,16,128]{2,0,1:T(8,128)S(1)}, f32[64,16,128]{2,0,1:T(8,128)}, u32[]{:S(2)}, u32[]{:S(2)}) collective-permute-start(f32[64,16,128]{2,0,1:T(8,128)S(1)} %broadcast_select_fusion.3), channel_id=1, source_target_pairs={{0,1},{1,2},{2,3},{3,4},{4,5},{5,6},{6,7},{7,8},{8,9},{9,10},{10,1... | collective-permute-start | bytes 1572872 | tf_op jit(solution)/shard_map/ppermute | solution.py:16
  178.5 1.8 copy.37
  180.3 3.6 %all-to-all-start = ((f32[8,2,128,128]{3,1,0,2:T(2,128)}), f32[8,2,128,128]{3,1,0,2:T(2,128)S(1)}, u32[]{:S(2)}, u32[]{:S(2)}) async-start(f32[8,2,128,128]{3,1,0,2:T(2,128)} %copy.37), calls=%async_computation | async-start | bytes 2097152 | tf_op jit(solution)/shard_map/all_to_all | solution.py:60
  184.0 1.7 collective-permute-start.5
  185.7 7.0 %collective-permute-start.6 = (f32[64,16,128]{2,0,1:T(8,128)S(1)}, f32[64,16,128]{2,0,1:T(8,128)}, u32[]{:S(2)}, u32[]{:S(2)}) collective-permute-start(f32[64,16,128]{2,0,1:T(8,128)S(1)} %broadcast_select_fusion.9), channel_id=1, source_target_pairs={{0,1},{1,2},{2,3},{3,4},{4,5},{5,6},{6,7},{7,8},{8,9},{9,10},{10,1... | collective-permute-start | bytes 1572872 | tf_op jit(solution)/shard_map/ppermute | solution.py:16
  192.7 1.3 collective-permute-done.11
  194.0 1.2 broadcast_select_fusion.4
  195.1 5.5 %collective-permute-start.12 = (f32[64,16,128]{2,0,1:T(8,128)S(1)}, f32[64,16,128]{2,0,1:T(8,128)S(1)}, u32[]{:S(2)}, u32[]{:S(2)}) collective-permute-start(f32[64,16,128]{2,0,1:T(8,128)S(1)} %broadcast_select_fusion.4), channel_id=1, source_target_pairs={{0,31},{1,0},{2,1},{3,2},{4,3},{5,4},{6,5},{7,6},{8,7},{9,8},{10,9... | collective-permute-start | bytes 1572872 | tf_op jit(solution)/shard_map/ppermute | solution.py:16
  200.6 5.0 %all-to-all-done = f32[8,2,128,128]{3,1,0,2:T(2,128)S(1)} async-done(((f32[8,2,128,128]{3,1,0,2:T(2,128)}), f32[8,2,128,128]{3,1,0,2:T(2,128)S(1)}, u32[]{:S(2)}, u32[]{:S(2)}) %all-to-all-start) | async-done | bytes 1048608 | tf_op jit(solution)/shard_map/all_to_all | solution.py:60
  206.6 9.3 %collective-permute-done.5 = f32[64,16,128]{2,0,1:T(8,128)S(1)} collective-permute-done((f32[64,16,128]{2,0,1:T(8,128)S(1)}, f32[64,16,128]{2,0,1:T(8,128)S(1)}, u32[]{:S(2)}, u32[]{:S(2)}) %collective-permute-start.5) | collective-permute-done | bytes 524320 | tf_op jit(solution)/shard_map/ppermute | solution.py:16
  215.9 10.1 %collective-permute-done.12 = f32[64,16,128]{2,0,1:T(8,128)S(1)} collective-permute-done((f32[64,16,128]{2,0,1:T(8,128)S(1)}, f32[64,16,128]{2,0,1:T(8,128)S(1)}, u32[]{:S(2)}, u32[]{:S(2)}) %collective-permute-start.12) | collective-permute-done | bytes 524320 | tf_op jit(solution)/shard_map/ppermute | solution.py:16
  226.0 1.7 add_bitcast_fusion.1
  227.9 1.2 fusion.3
  229.8 16.5 %all_to_all.51 = f32[64,2,16,128]{3,2,1,0:T(8,128)S(1)} all-to-all(f32[64,2,16,128]{3,2,1,0:T(8,128)S(1)} %copy.46), channel_id=1, replica_groups=mesh['tm'=8,'azim'=32] {'tm'}, dimensions={0} | all-to-all | bytes 2097152 | tf_op jit(solution)/shard_map/all_to_all | solution.py:97
  246.3 1.1 copy-done.3
  247.5 2.1 sub.12
  (52 shorter events, 8.0 us)
Async XLA Ops:
  0.0 200.6 %copy-start = (f32[1,16384]{1,0:T(1,128)S(1)}, f32[1,16384]{1,0:T(1,128)}, u32[]{:S(2)}) copy-start(f32[1,16384]{1,0:T(1,128)} %param.14) | copy-start | bytes 196612
  3.0 42.3 %all-to-all-start.1 = ((f32[8,2,128,128]{3,1,0,2:T(2,128)}), f32[8,2,128,128]{3,1,0,2:T(2,128)S(1)}, u32[]{:S(2)}, u32[]{:S(2)}) async-start(f32[8,2,128,128]{3,1,0,2:T(2,128)} %copy.42), calls=%async_computation.1 | async-start | bytes 2097152 | tf_op jit(solution)/shard_map/all_to_all | solution.py:53
  10.5 0.7 copy-start.5
  10.5 0.7 copy-start.6
  47.5 12.7 %copy-start.1 = (s32[32,5]{1,0:T(8,128)S(1)}, s32[32,5]{1,0:T(8,128)}, u32[]{:S(2)}) copy-start(s32[32,5]{1,0:T(8,128)} %constant.99.clone2.1) | copy-start | bytes 1924
  47.6 14.4 %collective-permute-start = (f32[64,16,128]{2,0,1:T(8,128)S(1)}, f32[64,16,128]{2,0,1:T(8,128)S(1)}, u32[]{:S(2)}, u32[]{:S(2)}) collective-permute-start(f32[64,16,128]{2,0,1:T(8,128)S(1)} %get-tuple-element.22), channel_id=1, source_target_pairs={{0,1},{1,2},{2,3},{3,4},{4,5},{5,6},{6,7},{7,8},{8,9},{9,10},{10,1... | collective-permute-start | bytes 1572872 | tf_op jit(solution)/shard_map/ppermute | solution.py:16
  53.2 21.5 %collective-permute-start.7 = (f32[64,16,128]{2,0,1:T(8,128)S(1)}, f32[64,16,128]{2,0,1:T(8,128)S(1)}, u32[]{:S(2)}, u32[]{:S(2)}) collective-permute-start(f32[64,16,128]{2,0,1:T(8,128)S(1)} %get-tuple-element.23), channel_id=1, source_target_pairs={{0,16},{1,17},{2,18},{3,19},{4,20},{5,21},{6,22},{7,23},{8,24},{9,... | collective-permute-start | bytes 1572872 | tf_op jit(solution)/shard_map/ppermute | solution.py:16
  60.2 0.7 copy-start.2
  74.9 25.7 %collective-permute-start.1 = (f32[64,16,128]{2,0,1:T(8,128)S(1)}, f32[64,16,128]{2,0,1:T(8,128)S(1)}, u32[]{:S(2)}, u32[]{:S(2)}) collective-permute-start(f32[64,16,128]{2,0,1:T(8,128)S(1)} %get-tuple-element.20), channel_id=1, source_target_pairs={{0,2},{1,3},{2,4},{3,5},{4,6},{5,7},{6,8},{7,9},{8,10},{9,11},{10,... | collective-permute-start | bytes 1572872 | tf_op jit(solution)/shard_map/ppermute | solution.py:16
  82.0 31.1 %collective-permute-start.8 = (f32[64,16,128]{2,0,1:T(8,128)S(1)}, f32[64,16,128]{2,0,1:T(8,128)S(1)}, u32[]{:S(2)}, u32[]{:S(2)}) collective-permute-start(f32[64,16,128]{2,0,1:T(8,128)S(1)} %get-tuple-element.21), channel_id=1, source_target_pairs={{0,8},{1,9},{2,10},{3,11},{4,12},{5,13},{6,14},{7,15},{8,16},{9,17... | collective-permute-start | bytes 1572872 | tf_op jit(solution)/shard_map/ppermute | solution.py:16
  100.7 23.6 %collective-permute-start.2 = (f32[64,16,128]{2,0,1:T(8,128)S(1)}, f32[64,16,128]{2,0,1:T(8,128)S(1)}, u32[]{:S(2)}, u32[]{:S(2)}) collective-permute-start(f32[64,16,128]{2,0,1:T(8,128)S(1)} %broadcast_select_fusion.6), channel_id=1, source_target_pairs={{0,4},{1,5},{2,6},{3,7},{4,8},{5,9},{6,10},{7,11},{8,12},{9,13},{1... | collective-permute-start | bytes 1572872 | tf_op jit(solution)/shard_map/ppermute | solution.py:16
  113.2 13.1 %collective-permute-start.9 = (f32[64,16,128]{2,0,1:T(8,128)S(1)}, f32[64,16,128]{2,0,1:T(8,128)S(1)}, u32[]{:S(2)}, u32[]{:S(2)}) collective-permute-start(f32[64,16,128]{2,0,1:T(8,128)S(1)} %broadcast_select_fusion.1), channel_id=1, source_target_pairs={{0,28},{1,29},{2,30},{3,31},{4,0},{5,1},{6,2},{7,3},{8,4},{9,5},{1... | collective-permute-start | bytes 1572872 | tf_op jit(solution)/shard_map/ppermute | solution.py:16
  124.4 25.5 %collective-permute-start.3 = (f32[64,16,128]{2,0,1:T(8,128)S(1)}, f32[64,16,128]{2,0,1:T(8,128)S(1)}, u32[]{:S(2)}, u32[]{:S(2)}) collective-permute-start(f32[64,16,128]{2,0,1:T(8,128)S(1)} %broadcast_select_fusion.7), channel_id=1, source_target_pairs={{0,24},{1,25},{2,26},{3,27},{4,28},{5,29},{6,30},{7,31},{8,0},{9,1... | collective-permute-start | bytes 1572872 | tf_op jit(solution)/shard_map/ppermute | solution.py:16
  126.5 25.6 %collective-permute-start.10 = (f32[64,16,128]{2,0,1:T(8,128)S(1)}, f32[64,16,128]{2,0,1:T(8,128)S(1)}, u32[]{:S(2)}, u32[]{:S(2)}) collective-permute-start(f32[64,16,128]{2,0,1:T(8,128)S(1)} %broadcast_select_fusion.2), channel_id=1, source_target_pairs={{0,2},{1,3},{2,4},{3,5},{4,6},{5,7},{6,8},{7,9},{8,10},{9,11},{10,... | collective-permute-start | bytes 1572872 | tf_op jit(solution)/shard_map/ppermute | solution.py:16
  150.0 28.5 %copy-start.4 = (f32[8,2,1,16384]{3,2,1,0:T(1,128)S(1)}, f32[8,2,1,16384]{3,2,1,0:T(1,128)}, u32[]{:S(2)}) copy-start(f32[8,2,1,16384]{3,2,1,0:T(1,128)} %param.11) | copy-start | bytes 3145732
  150.0 33.8 %collective-permute-start.4 = (f32[64,16,128]{2,0,1:T(8,128)S(1)}, f32[64,16,128]{2,0,1:T(8,128)S(1)}, u32[]{:S(2)}, u32[]{:S(2)}) collective-permute-start(f32[64,16,128]{2,0,1:T(8,128)S(1)} %broadcast_select_fusion.8), channel_id=1, source_target_pairs={{0,16},{1,17},{2,18},{3,19},{4,20},{5,21},{6,22},{7,23},{8,24},{9,... | collective-permute-start | bytes 1572872 | tf_op jit(solution)/shard_map/ppermute | solution.py:16
  152.3 41.7 %collective-permute-start.11 = (f32[64,16,128]{2,0,1:T(8,128)S(1)}, f32[64,16,128]{2,0,1:T(8,128)}, u32[]{:S(2)}, u32[]{:S(2)}) collective-permute-start(f32[64,16,128]{2,0,1:T(8,128)S(1)} %broadcast_select_fusion.3), channel_id=1, source_target_pairs={{0,1},{1,2},{2,3},{3,4},{4,5},{5,6},{6,7},{7,8},{8,9},{9,10},{10,1... | collective-permute-start | bytes 1572872 | tf_op jit(solution)/shard_map/ppermute | solution.py:16
  180.3 25.4 %all-to-all-start = ((f32[8,2,128,128]{3,1,0,2:T(2,128)}), f32[8,2,128,128]{3,1,0,2:T(2,128)S(1)}, u32[]{:S(2)}, u32[]{:S(2)}) async-start(f32[8,2,128,128]{3,1,0,2:T(2,128)} %copy.37), calls=%async_computation | async-start | bytes 2097152 | tf_op jit(solution)/shard_map/all_to_all | solution.py:60
  184.0 31.9 %collective-permute-start.5 = (f32[64,16,128]{2,0,1:T(8,128)S(1)}, f32[64,16,128]{2,0,1:T(8,128)S(1)}, u32[]{:S(2)}, u32[]{:S(2)}) collective-permute-start(f32[64,16,128]{2,0,1:T(8,128)S(1)} %broadcast_select_fusion.9), channel_id=1, source_target_pairs={{0,31},{1,0},{2,1},{3,2},{4,3},{5,4},{6,5},{7,6},{8,7},{9,8},{10,9... | collective-permute-start | bytes 1572872 | tf_op jit(solution)/shard_map/ppermute | solution.py:16
  185.7 30.2 %collective-permute-start.6 = (f32[64,16,128]{2,0,1:T(8,128)S(1)}, f32[64,16,128]{2,0,1:T(8,128)}, u32[]{:S(2)}, u32[]{:S(2)}) collective-permute-start(f32[64,16,128]{2,0,1:T(8,128)S(1)} %broadcast_select_fusion.9), channel_id=1, source_target_pairs={{0,1},{1,2},{2,3},{3,4},{4,5},{5,6},{6,7},{7,8},{8,9},{9,10},{10,1... | collective-permute-start | bytes 1572872 | tf_op jit(solution)/shard_map/ppermute | solution.py:16
  195.1 30.9 %collective-permute-start.12 = (f32[64,16,128]{2,0,1:T(8,128)S(1)}, f32[64,16,128]{2,0,1:T(8,128)S(1)}, u32[]{:S(2)}, u32[]{:S(2)}) collective-permute-start(f32[64,16,128]{2,0,1:T(8,128)S(1)} %broadcast_select_fusion.4), channel_id=1, source_target_pairs={{0,31},{1,0},{2,1},{3,2},{4,3},{5,4},{6,5},{7,6},{8,7},{9,8},{10,9... | collective-permute-start | bytes 1572872 | tf_op jit(solution)/shard_map/ppermute | solution.py:16
  200.6 25.4 %collective-permute-start.13 = (f32[64,16,128]{2,0,1:T(8,128)S(1)}, f32[64,16,128]{2,0,1:T(8,128)}, u32[]{:S(2)}, u32[]{:S(2)}) collective-permute-start(f32[64,16,128]{2,0,1:T(8,128)S(1)} %broadcast_select_fusion.4), channel_id=1, source_target_pairs={{0,1},{1,2},{2,3},{3,4},{4,5},{5,6},{6,7},{7,8},{8,9},{9,10},{10,1... | collective-permute-start | bytes 1572872 | tf_op jit(solution)/shard_map/ppermute | solution.py:16
  246.2 1.2 copy-start.3
where the time goes:
time: 250 us
  starting transfers between devices  95.6 us (38%)
  waiting for transfers between devices  83.4 us (33%)
  blocking collectives  50.5 us (20%)
  local copies, waits for them, and re-layouts  10.1 us (4%)
  other arithmetic  6.77 us (3%)
  matrix products  2.96 us (1%)
    ppermute x14, starting transfers between devices, shifted(): return lax.ppermute(value, axis, pairs)  84.5 us
    ppermute x14, waiting for transfers between devices, shifted(): return lax.ppermute(value, axis, pairs)  78.3 us
    all_gather x1, blocking collectives, body(): small = lax.all_gather(small, 'tm', tiled=True).astype(jnp.int32)  34 us
    all_to_all x1, blocking collectives, body(): lax.all_to_all(summed, 'tm', split_axis=0, concat_axis=2, tiled=True)  16.5 us
    all_to_all x1, starting transfers between devices, body(): lax.all_to_all(rotor_coeffs.reshape(local_c, comp, rows, LANES), 'tm', sp...  7.48 us
    all_to_all x1, waiting for transfers between devices, body(): lax.all_to_all(mortar_weights.reshape(local_j, sten, rows, LANES), 'tm',...  5.02 us
  transfers between devices with their start and end apart: 16, of which 10 were waited for; matrix products, arithmetic and copies ran while one was open for 3% of the time, Pallas kernels for 0%

commit v1 on v0

--- a/solution.py
+++ b/solution.py
@@ -50,12 +50,18 @@
     rows = nodes // LANES
     parts = lax.axis_size("tm")
     chunk = rows // parts
-    coeffs = lax.all_to_all(
-        rotor_coeffs.reshape(local_c, comp, rows, LANES),
-        "tm",
-        split_axis=2,
-        concat_axis=0,
-        tiled=True,
+    coeffs = jnp.concatenate(
+        lax.all_to_all(
+            jnp.stack(
+                jnp.split(
+                    rotor_coeffs.reshape(local_c, comp, rows, LANES), lax.axis_size("tm"), axis=2
+                )
+            ),
+            "tm",
+            0,
+            0,
+        ),
+        axis=0,
     )
     weights = lax.all_to_all(
         mortar_weights.reshape(local_j, sten, rows, LANES),

time: 250 us -> 249 us (level)
    reshape x1 -> x0, local copies, waits for them, and re-layouts: 3.04 us -> none  [body(): rotor_coeffs.reshape(local_c, comp, rows, LANES)]
where the time goes in v1:
time: 249 us; the launch traced here: 248 us
  starting transfers between devices  95.1 us (38%)
  waiting for transfers between devices  83.8 us (34%)
  blocking collectives  50.4 us (20%)
  local copies, waits for them, and re-layouts  9.53 us (4%)
  other arithmetic  6.77 us (3%)
    ppermute x14, starting transfers between devices, shifted(): return lax.ppermute(value, axis, pairs)  84.1 us
    ppermute x14, waiting for transfers between devices, shifted(): return lax.ppermute(value, axis, pairs)  78.5 us
    all_gather x1, blocking collectives, body(): small = lax.all_gather(small, 'tm', tiled=True).astype(jnp.int32)  34 us
    all_to_all x1, blocking collectives, body(): lax.all_to_all(summed, 'tm', split_axis=0, concat_axis=2, tiled=True)  16.4 us
    all_to_all x1, starting transfers between devices, body(): lax.all_to_all(jnp.stack(jnp.split(rotor_coeffs.reshape(local_c, comp, ro...  7.48 us
    all_to_all x1, waiting for transfers between devices, body(): lax.all_to_all(mortar_weights.reshape(local_j, sten, rows, LANES), 'tm',...  5.38 us
  transfers between devices with their start and end apart: 16, of which 10 were waited for; matrix products, arithmetic and copies ran while one was open for 3% of the time, Pallas kernels for 0%

profile of v1, /device:TPU:1, one launch (start us, length us, event | category | flops | bytes accessed | tf_op | source)
XLA Modules:
  0.0 248.4 jit_solution(12084259370579526650)
XLA Ops:
  0.0 1.4 fusion.48
  1.6 1.3 copy.55
  2.9 7.5 %all-to-all-start.1 = ((f32[8,8,2,16,128]{4,1,3,2,0:T(8,128)}), f32[8,8,2,16,128]{4,1,3,2,0:T(8,128)S(1)}, u32[]{:S(2)}, u32[]{:S(2)}) async-start(f32[8,8,2,16,128]{4,1,3,2,0:T(8,128)} %copy.55), calls=%async_computation.1 | async-start | bytes 2097152 | tf_op jit(solution)/shard_map/all_to_all | solution.py:54
  11.0 34.0 %all-gather = f32[8,8,3]{1,2,0:T(4,128)S(1)} all-gather(f32[1,8,3]{1,2,0:T(4,128)S(1)} %fusion.33), channel_id=1, replica_groups=mesh['tm'=8,'azim'=32] {'tm'}, dimensions={0}, use_global_device_ids=true | all-gather | bytes 864 | tf_op jit(solution)/shard_map/all_gather | solution.py:74
  45.2 1.2 fusion
  46.5 5.6 %collective-permute-start = (f32[64,16,128]{2,0,1:T(8,128)S(1)}, f32[64,16,128]{2,0,1:T(8,128)S(1)}, u32[]{:S(2)}, u32[]{:S(2)}) collective-permute-start(f32[64,16,128]{2,0,1:T(8,128)S(1)} %get-tuple-element.22), channel_id=1, source_target_pairs={{0,1},{1,2},{2,3},{3,4},{4,5},{5,6},{6,7},{7,8},{8,9},{9,10},{10,1... | collective-permute-start | bytes 1572872 | tf_op jit(solution)/shard_map/ppermute | solution.py:16
  52.2 6.9 %collective-permute-start.7 = (f32[64,16,128]{2,0,1:T(8,128)S(1)}, f32[64,16,128]{2,0,1:T(8,128)S(1)}, u32[]{:S(2)}, u32[]{:S(2)}) collective-permute-start(f32[64,16,128]{2,0,1:T(8,128)S(1)} %get-tuple-element.23), channel_id=1, source_target_pairs={{0,16},{1,17},{2,18},{3,19},{4,20},{5,21},{6,22},{7,23},{8,24},{9,... | collective-permute-start | bytes 1572872 | tf_op jit(solution)/shard_map/ppermute | solution.py:16
  60.9 12.7 %collective-permute-done.7 = f32[64,16,128]{2,0,1:T(8,128)S(1)} collective-permute-done((f32[64,16,128]{2,0,1:T(8,128)S(1)}, f32[64,16,128]{2,0,1:T(8,128)S(1)}, u32[]{:S(2)}, u32[]{:S(2)}) %collective-permute-start.7) | collective-permute-done | bytes 524320 | tf_op jit(solution)/shard_map/ppermute | solution.py:16
  73.8 7.1 %collective-permute-start.1 = (f32[64,16,128]{2,0,1:T(8,128)S(1)}, f32[64,16,128]{2,0,1:T(8,128)S(1)}, u32[]{:S(2)}, u32[]{:S(2)}) collective-permute-start(f32[64,16,128]{2,0,1:T(8,128)S(1)} %get-tuple-element.20), channel_id=1, source_target_pairs={{0,2},{1,3},{2,4},{3,5},{4,6},{5,7},{6,8},{7,9},{8,10},{9,11},{10,... | collective-permute-start | bytes 1572872 | tf_op jit(solution)/shard_map/ppermute | solution.py:16
  81.0 9.7 %collective-permute-start.8 = (f32[64,16,128]{2,0,1:T(8,128)S(1)}, f32[64,16,128]{2,0,1:T(8,128)S(1)}, u32[]{:S(2)}, u32[]{:S(2)}) collective-permute-start(f32[64,16,128]{2,0,1:T(8,128)S(1)} %get-tuple-element.21), channel_id=1, source_target_pairs={{0,8},{1,9},{2,10},{3,11},{4,12},{5,13},{6,14},{7,15},{8,16},{9,17... | collective-permute-start | bytes 1572872 | tf_op jit(solution)/shard_map/ppermute | solution.py:16
  90.6 8.9 %collective-permute-done.1 = f32[64,16,128]{2,0,1:T(8,128)S(1)} collective-permute-done((f32[64,16,128]{2,0,1:T(8,128)S(1)}, f32[64,16,128]{2,0,1:T(8,128)S(1)}, u32[]{:S(2)}, u32[]{:S(2)}) %collective-permute-start.1) | collective-permute-done | bytes 524320 | tf_op jit(solution)/shard_map/ppermute | solution.py:16
  100.7 11.3 %collective-permute-done.8 = f32[64,16,128]{2,0,1:T(8,128)S(1)} collective-permute-done((f32[64,16,128]{2,0,1:T(8,128)S(1)}, f32[64,16,128]{2,0,1:T(8,128)S(1)}, u32[]{:S(2)}, u32[]{:S(2)}) %collective-permute-start.8) | collective-permute-done | bytes 524320 | tf_op jit(solution)/shard_map/ppermute | solution.py:16
  112.3 11.0 %collective-permute-done.2 = f32[64,16,128]{2,0,1:T(8,128)S(1)} collective-permute-done((f32[64,16,128]{2,0,1:T(8,128)S(1)}, f32[64,16,128]{2,0,1:T(8,128)S(1)}, u32[]{:S(2)}, u32[]{:S(2)}) %collective-permute-start.2) | collective-permute-done | bytes 524320 | tf_op jit(solution)/shard_map/ppermute | solution.py:16
  125.5 10.6 %collective-permute-start.10 = (f32[64,16,128]{2,0,1:T(8,128)S(1)}, f32[64,16,128]{2,0,1:T(8,128)S(1)}, u32[]{:S(2)}, u32[]{:S(2)}) collective-permute-start(f32[64,16,128]{2,0,1:T(8,128)S(1)} %broadcast_select_fusion.2), channel_id=1, source_target_pairs={{0,2},{1,3},{2,4},{3,5},{4,6},{5,7},{6,8},{7,9},{8,10},{9,11},{10,... | collective-permute-start | bytes 1572872 | tf_op jit(solution)/shard_map/ppermute | solution.py:16
  136.0 12.8 %collective-permute-done.3 = f32[64,16,128]{2,0,1:T(8,128)S(1)} collective-permute-done((f32[64,16,128]{2,0,1:T(8,128)S(1)}, f32[64,16,128]{2,0,1:T(8,128)S(1)}, u32[]{:S(2)}, u32[]{:S(2)}) %collective-permute-start.3) | collective-permute-done | bytes 524320 | tf_op jit(solution)/shard_map/ppermute | solution.py:16
  149.0 2.1 collective-permute-start.4
  151.2 26.0 %collective-permute-start.11 = (f32[64,16,128]{2,0,1:T(8,128)S(1)}, f32[64,16,128]{2,0,1:T(8,128)}, u32[]{:S(2)}, u32[]{:S(2)}) collective-permute-start(f32[64,16,128]{2,0,1:T(8,128)S(1)} %broadcast_select_fusion.3), channel_id=1, source_target_pairs={{0,1},{1,2},{2,3},{3,4},{4,5},{5,6},{6,7},{7,8},{8,9},{9,10},{10,1... | collective-permute-start | bytes 1572872 | tf_op jit(solution)/shard_map/ppermute | solution.py:16
  177.2 1.8 copy.50
  179.0 3.6 %all-to-all-start = ((f32[8,2,128,128]{3,1,0,2:T(2,128)}), f32[8,2,128,128]{3,1,0,2:T(2,128)S(1)}, u32[]{:S(2)}, u32[]{:S(2)}) async-start(f32[8,2,128,128]{3,1,0,2:T(2,128)} %copy.50), calls=%async_computation | async-start | bytes 2097152 | tf_op jit(solution)/shard_map/all_to_all | solution.py:66
  182.7 2.1 collective-permute-start.5
  184.8 7.0 %collective-permute-start.6 = (f32[64,16,128]{2,0,1:T(8,128)S(1)}, f32[64,16,128]{2,0,1:T(8,128)}, u32[]{:S(2)}, u32[]{:S(2)}) collective-permute-start(f32[64,16,128]{2,0,1:T(8,128)S(1)} %broadcast_select_fusion.9), channel_id=1, source_target_pairs={{0,1},{1,2},{2,3},{3,4},{4,5},{5,6},{6,7},{7,8},{8,9},{9,10},{10,1... | collective-permute-start | bytes 1572872 | tf_op jit(solution)/shard_map/ppermute | solution.py:16
  191.8 1.6 collective-permute-done.11
  193.3 1.2 broadcast_select_fusion.4
  194.5 4.9 %collective-permute-start.12 = (f32[64,16,128]{2,0,1:T(8,128)S(1)}, f32[64,16,128]{2,0,1:T(8,128)S(1)}, u32[]{:S(2)}, u32[]{:S(2)}) collective-permute-start(f32[64,16,128]{2,0,1:T(8,128)S(1)} %broadcast_select_fusion.4), channel_id=1, source_target_pairs={{0,31},{1,0},{2,1},{3,2},{4,3},{5,4},{6,5},{7,6},{8,7},{9,8},{10,9... | collective-permute-start | bytes 1572872 | tf_op jit(solution)/shard_map/ppermute | solution.py:16
  199.4 5.4 %all-to-all-done = f32[8,2,128,128]{3,1,0,2:T(2,128)S(1)} async-done(((f32[8,2,128,128]{3,1,0,2:T(2,128)}), f32[8,2,128,128]{3,1,0,2:T(2,128)S(1)}, u32[]{:S(2)}, u32[]{:S(2)}) %all-to-all-start) | async-done | bytes 1048608 | tf_op jit(solution)/shard_map/all_to_all | solution.py:66
  205.7 9.2 %collective-permute-done.5 = f32[64,16,128]{2,0,1:T(8,128)S(1)} collective-permute-done((f32[64,16,128]{2,0,1:T(8,128)S(1)}, f32[64,16,128]{2,0,1:T(8,128)S(1)}, u32[]{:S(2)}, u32[]{:S(2)}) %collective-permute-start.5) | collective-permute-done | bytes 524320 | tf_op jit(solution)/shard_map/ppermute | solution.py:16
  214.9 10.0 %collective-permute-done.12 = f32[64,16,128]{2,0,1:T(8,128)S(1)} collective-permute-done((f32[64,16,128]{2,0,1:T(8,128)S(1)}, f32[64,16,128]{2,0,1:T(8,128)S(1)}, u32[]{:S(2)}, u32[]{:S(2)}) %collective-permute-start.12) | collective-permute-done | bytes 524320 | tf_op jit(solution)/shard_map/ppermute | solution.py:16
  225.0 1.7 add_bitcast_fusion.1
  226.9 1.2 fusion.3
  228.7 16.4 %all_to_all.38 = f32[64,2,16,128]{3,2,1,0:T(8,128)S(1)} all-to-all(f32[64,2,16,128]{3,2,1,0:T(8,128)S(1)} %copy.58), channel_id=1, replica_groups=mesh['tm'=8,'azim'=32] {'tm'}, dimensions={0} | all-to-all | bytes 2097152 | tf_op jit(solution)/shard_map/all_to_all | solution.py:103
  245.2 1.1 copy-done.3
  246.3 2.1 sub.12
  (60 shorter events, 8.8 us)
Async XLA Ops:
  0.0 199.4 %copy-start = (f32[1,16384]{1,0:T(1,128)S(1)}, f32[1,16384]{1,0:T(1,128)}, u32[]{:S(2)}) copy-start(f32[1,16384]{1,0:T(1,128)} %param.14) | copy-start | bytes 196612
  2.9 42.3 %all-to-all-start.1 = ((f32[8,8,2,16,128]{4,1,3,2,0:T(8,128)}), f32[8,8,2,16,128]{4,1,3,2,0:T(8,128)S(1)}, u32[]{:S(2)}, u32[]{:S(2)}) async-start(f32[8,8,2,16,128]{4,1,3,2,0:T(8,128)} %copy.55), calls=%async_computation.1 | async-start | bytes 2097152 | tf_op jit(solution)/shard_map/all_to_all | solution.py:54
  10.3 0.7 copy-start.5
  10.3 0.7 copy-start.6
  46.4 12.7 %copy-start.1 = (s32[32,5]{1,0:T(8,128)S(1)}, s32[32,5]{1,0:T(8,128)}, u32[]{:S(2)}) copy-start(s32[32,5]{1,0:T(8,128)} %constant.99.clone2.1) | copy-start | bytes 1924
  46.5 14.4 %collective-permute-start = (f32[64,16,128]{2,0,1:T(8,128)S(1)}, f32[64,16,128]{2,0,1:T(8,128)S(1)}, u32[]{:S(2)}, u32[]{:S(2)}) collective-permute-start(f32[64,16,128]{2,0,1:T(8,128)S(1)} %get-tuple-element.22), channel_id=1, source_target_pairs={{0,1},{1,2},{2,3},{3,4},{4,5},{5,6},{6,7},{7,8},{8,9},{9,10},{10,1... | collective-permute-start | bytes 1572872 | tf_op jit(solution)/shard_map/ppermute | solution.py:16
  52.2 21.5 %collective-permute-start.7 = (f32[64,16,128]{2,0,1:T(8,128)S(1)}, f32[64,16,128]{2,0,1:T(8,128)S(1)}, u32[]{:S(2)}, u32[]{:S(2)}) collective-permute-start(f32[64,16,128]{2,0,1:T(8,128)S(1)} %get-tuple-element.23), channel_id=1, source_target_pairs={{0,16},{1,17},{2,18},{3,19},{4,20},{5,21},{6,22},{7,23},{8,24},{9,... | collective-permute-start | bytes 1572872 | tf_op jit(solution)/shard_map/ppermute | solution.py:16
  59.1 0.7 copy-start.2
  73.8 25.7 %collective-permute-start.1 = (f32[64,16,128]{2,0,1:T(8,128)S(1)}, f32[64,16,128]{2,0,1:T(8,128)S(1)}, u32[]{:S(2)}, u32[]{:S(2)}) collective-permute-start(f32[64,16,128]{2,0,1:T(8,128)S(1)} %get-tuple-element.20), channel_id=1, source_target_pairs={{0,2},{1,3},{2,4},{3,5},{4,6},{5,7},{6,8},{7,9},{8,10},{9,11},{10,... | collective-permute-start | bytes 1572872 | tf_op jit(solution)/shard_map/ppermute | solution.py:16
  81.0 31.1 %collective-permute-start.8 = (f32[64,16,128]{2,0,1:T(8,128)S(1)}, f32[64,16,128]{2,0,1:T(8,128)S(1)}, u32[]{:S(2)}, u32[]{:S(2)}) collective-permute-start(f32[64,16,128]{2,0,1:T(8,128)S(1)} %get-tuple-element.21), channel_id=1, source_target_pairs={{0,8},{1,9},{2,10},{3,11},{4,12},{5,13},{6,14},{7,15},{8,16},{9,17... | collective-permute-start | bytes 1572872 | tf_op jit(solution)/shard_map/ppermute | solution.py:16
  99.7 23.6 %collective-permute-start.2 = (f32[64,16,128]{2,0,1:T(8,128)S(1)}, f32[64,16,128]{2,0,1:T(8,128)S(1)}, u32[]{:S(2)}, u32[]{:S(2)}) collective-permute-start(f32[64,16,128]{2,0,1:T(8,128)S(1)} %broadcast_select_fusion.6), channel_id=1, source_target_pairs={{0,4},{1,5},{2,6},{3,7},{4,8},{5,9},{6,10},{7,11},{8,12},{9,13},{1... | collective-permute-start | bytes 1572872 | tf_op jit(solution)/shard_map/ppermute | solution.py:16
  112.2 13.1 %collective-permute-start.9 = (f32[64,16,128]{2,0,1:T(8,128)S(1)}, f32[64,16,128]{2,0,1:T(8,128)S(1)}, u32[]{:S(2)}, u32[]{:S(2)}) collective-permute-start(f32[64,16,128]{2,0,1:T(8,128)S(1)} %broadcast_select_fusion.1), channel_id=1, source_target_pairs={{0,28},{1,29},{2,30},{3,31},{4,0},{5,1},{6,2},{7,3},{8,4},{9,5},{1... | collective-permute-start | bytes 1572872 | tf_op jit(solution)/shard_map/ppermute | solution.py:16
  123.4 25.5 %collective-permute-start.3 = (f32[64,16,128]{2,0,1:T(8,128)S(1)}, f32[64,16,128]{2,0,1:T(8,128)S(1)}, u32[]{:S(2)}, u32[]{:S(2)}) collective-permute-start(f32[64,16,128]{2,0,1:T(8,128)S(1)} %broadcast_select_fusion.7), channel_id=1, source_target_pairs={{0,24},{1,25},{2,26},{3,27},{4,28},{5,29},{6,30},{7,31},{8,0},{9,1... | collective-permute-start | bytes 1572872 | tf_op jit(solution)/shard_map/ppermute | solution.py:16
  125.5 25.6 %collective-permute-start.10 = (f32[64,16,128]{2,0,1:T(8,128)S(1)}, f32[64,16,128]{2,0,1:T(8,128)S(1)}, u32[]{:S(2)}, u32[]{:S(2)}) collective-permute-start(f32[64,16,128]{2,0,1:T(8,128)S(1)} %broadcast_select_fusion.2), channel_id=1, source_target_pairs={{0,2},{1,3},{2,4},{3,5},{4,6},{5,7},{6,8},{7,9},{8,10},{9,11},{10,... | collective-permute-start | bytes 1572872 | tf_op jit(solution)/shard_map/ppermute | solution.py:16
  149.0 28.2 %copy-start.4 = (f32[8,2,1,16384]{3,2,1,0:T(1,128)S(1)}, f32[8,2,1,16384]{3,2,1,0:T(1,128)}, u32[]{:S(2)}) copy-start(f32[8,2,1,16384]{3,2,1,0:T(1,128)} %param.11) | copy-start | bytes 3145732
  149.0 33.6 %collective-permute-start.4 = (f32[64,16,128]{2,0,1:T(8,128)S(1)}, f32[64,16,128]{2,0,1:T(8,128)S(1)}, u32[]{:S(2)}, u32[]{:S(2)}) collective-permute-start(f32[64,16,128]{2,0,1:T(8,128)S(1)} %broadcast_select_fusion.8), channel_id=1, source_target_pairs={{0,16},{1,17},{2,18},{3,19},{4,20},{5,21},{6,22},{7,23},{8,24},{9,... | collective-permute-start | bytes 1572872 | tf_op jit(solution)/shard_map/ppermute | solution.py:16
  151.2 42.1 %collective-permute-start.11 = (f32[64,16,128]{2,0,1:T(8,128)S(1)}, f32[64,16,128]{2,0,1:T(8,128)}, u32[]{:S(2)}, u32[]{:S(2)}) collective-permute-start(f32[64,16,128]{2,0,1:T(8,128)S(1)} %broadcast_select_fusion.3), channel_id=1, source_target_pairs={{0,1},{1,2},{2,3},{3,4},{4,5},{5,6},{6,7},{7,8},{8,9},{9,10},{10,1... | collective-permute-start | bytes 1572872 | tf_op jit(solution)/shard_map/ppermute | solution.py:16
  179.0 25.8 %all-to-all-start = ((f32[8,2,128,128]{3,1,0,2:T(2,128)}), f32[8,2,128,128]{3,1,0,2:T(2,128)S(1)}, u32[]{:S(2)}, u32[]{:S(2)}) async-start(f32[8,2,128,128]{3,1,0,2:T(2,128)} %copy.50), calls=%async_computation | async-start | bytes 2097152 | tf_op jit(solution)/shard_map/all_to_all | solution.py:66
  182.7 32.2 %collective-permute-start.5 = (f32[64,16,128]{2,0,1:T(8,128)S(1)}, f32[64,16,128]{2,0,1:T(8,128)S(1)}, u32[]{:S(2)}, u32[]{:S(2)}) collective-permute-start(f32[64,16,128]{2,0,1:T(8,128)S(1)} %broadcast_select_fusion.9), channel_id=1, source_target_pairs={{0,31},{1,0},{2,1},{3,2},{4,3},{5,4},{6,5},{7,6},{8,7},{9,8},{10,9... | collective-permute-start | bytes 1572872 | tf_op jit(solution)/shard_map/ppermute | solution.py:16
  184.8 30.1 %collective-permute-start.6 = (f32[64,16,128]{2,0,1:T(8,128)S(1)}, f32[64,16,128]{2,0,1:T(8,128)}, u32[]{:S(2)}, u32[]{:S(2)}) collective-permute-start(f32[64,16,128]{2,0,1:T(8,128)S(1)} %broadcast_select_fusion.9), channel_id=1, source_target_pairs={{0,1},{1,2},{2,3},{3,4},{4,5},{5,6},{6,7},{7,8},{8,9},{9,10},{10,1... | collective-permute-start | bytes 1572872 | tf_op jit(solution)/shard_map/ppermute | solution.py:16
  194.5 30.4 %collective-permute-start.12 = (f32[64,16,128]{2,0,1:T(8,128)S(1)}, f32[64,16,128]{2,0,1:T(8,128)S(1)}, u32[]{:S(2)}, u32[]{:S(2)}) collective-permute-start(f32[64,16,128]{2,0,1:T(8,128)S(1)} %broadcast_select_fusion.4), channel_id=1, source_target_pairs={{0,31},{1,0},{2,1},{3,2},{4,3},{5,4},{6,5},{7,6},{8,7},{9,8},{10,9... | collective-permute-start | bytes 1572872 | tf_op jit(solution)/shard_map/ppermute | solution.py:16
  199.4 25.6 %collective-permute-start.13 = (f32[64,16,128]{2,0,1:T(8,128)S(1)}, f32[64,16,128]{2,0,1:T(8,128)}, u32[]{:S(2)}, u32[]{:S(2)}) collective-permute-start(f32[64,16,128]{2,0,1:T(8,128)S(1)} %broadcast_select_fusion.4), channel_id=1, source_target_pairs={{0,1},{1,2},{2,3},{3,4},{4,5},{5,6},{6,7},{7,8},{8,9},{9,10},{10,1... | collective-permute-start | bytes 1572872 | tf_op jit(solution)/shard_map/ppermute | solution.py:16
  245.1 1.2 copy-start.3
